TPU v7x, 256 devices: a whole 4x4x8 slice. The times are simulated.
256 devices in a mesh: depth: 8 (over z), board: 32 (over x, y, core).
Axes of the slice: x: 4, y: 4, z: 8, core: 2. Of those that a mesh axis runs over, the one named last changes fastest.
Arguments:
- root_reach: float32 [32, 1326], P('board'), may hold values from 0.05 to 1
- opp_strat: float32 [32, 8, 16, 1326], P('board', 'depth'), may hold values from 0.55 to 1
- own_strat: float32 [32, 8, 16, 1326], P('board', 'depth'), may hold values from 0.55 to 1
- parent: int32 [8, 16], P('depth'), may hold values from 0 to 15
- pot: float32 [32, 8, 16], P('board', 'depth'), may hold values from 1 to 8
- hand_cards: int32 [1326, 2], replicated, may hold values from 0 to 51, as said below
- river_card: int32 [32, 26], P('board'), may hold values from 0 to 51, as said below
- board_owner: int32 [32, 26], P('board'), may hold values from 0 to 31
- board_slot: int32 [32, 26], P('board'), may hold values from 0 to 1, as said below
- river_strength: float32 [32, 32, 2, 1326], P('board'), may hold values from -6 to 6
Outputs:
- node_value: float32 [32, 8, 16, 1326], P('board', 'depth')
Inputs may be any that keep to these rules, and one draw needn't show every extreme that they name: `hand_cards`: each row holds two different cards, the lower first; no two rows are the same hand. `river_card`: the river cards of one front are distinct. Within one row of board_owner and board_slot the pairs are distinct; in every row some owner takes all 2 slots.
All inputs are finite; a program needn't handle non-finite values.
Results may differ from a plain program's by a relative error of at most 0.0003.
Values may be sent and summed in bfloat16 or wider, within the bound.
No kernel may reach another device: no remote copies, remote signals or barrier semaphores. Data moves between devices by JAX's collectives and lax.ppermute only.
A program may use at most 64 MiB of HBM per device.

v0:
```python
import jax
import jax.numpy as jnp
from jax import lax
from jax.sharding import PartitionSpec as P


def in_one_piece(arrays, axis, dim, along):
    widths = [a.shape[along] for a in arrays]
    both = jnp.concatenate(arrays, axis=along)
    filled = lax.all_gather(both, axis, axis=dim, tiled=True)
    return tuple(jnp.split(filled, [sum(widths[:k]) for k in range(1, len(widths))], axis=along))


def joined_along(parts, dim):
    dims = list(parts.shape[1:])
    dims[dim] *= parts.shape[0]
    return jnp.moveaxis(parts, 0, dim).reshape(dims)


def sent_to_all(x, axis):
    copies = jnp.broadcast_to(x, (lax.axis_size(axis), *x.shape))
    return lax.all_to_all(copies, axis, split_axis=0, concat_axis=0, tiled=True)


def collect(x, axis, dim):
    return joined_along(sent_to_all(x, axis), dim)


def side_by_side(arrays, axis, dim, along):
    both = jnp.concatenate(arrays, axis=along)
    filled, at, done = (collect(both, axis, dim), 0, [])
    for a in arrays:
        done.append(lax.slice_in_dim(filled, at, at + a.shape[along], axis=along))
        at += a.shape[along]
    return tuple(done)


def compatible_table(hand_cards):
    deck = jnp.arange(52, dtype=jnp.int32)
    onehot_cards = (
        (hand_cards[:, 0:1] == deck[None, :]) | (hand_cards[:, 1:2] == deck[None, :])
    ).astype(jnp.bfloat16)
    intersection = lax.dot_general(
        onehot_cards, onehot_cards, (((1,), (1,)), ((), ())), preferred_element_type=jnp.float32
    )
    return (intersection < 0.5).astype(jnp.bfloat16)


def alive_rows(hand_cards, river_row):
    missing = (hand_cards[None, :, 0] != river_row[:, None]) & (
        hand_cards[None, :, 1] != river_row[:, None]
    )
    return missing.astype(jnp.float32)


def showdown_block(strength, reach_rows, compatible):
    sign_table = jnp.sign(strength[:, None] - strength[None, :]).astype(jnp.bfloat16) * compatible
    return lax.dot_general(
        reach_rows, sign_table, (((1,), (1,)), ((), ())), preferred_element_type=jnp.float32
    )


def settle_boards(strengths, reach_boards, compatible):

    def settle_board(inputs):
        return showdown_block(inputs[0], inputs[1], compatible)

    return lax.map(settle_board, (strengths, reach_boards))


def choose_parent(selector, rows):
    return jnp.dot(
        selector, rows, precision=lax.Precision.HIGHEST, preferred_element_type=jnp.float32
    )


def lift_to_parents(selector, rows):
    return lax.dot_general(
        selector,
        rows,
        (((0,), (0,)), ((), ())),
        precision=lax.Precision.HIGHEST,
        preferred_element_type=jnp.float32,
    )


def body(
    root_reach,
    opp_strat,
    own_strat,
    parent,
    pot,
    hand_cards,
    river_card,
    board_owner,
    board_slot,
    river_strength,
):
    hand_count = root_reach.shape[1]
    node_count = opp_strat.shape[2]
    rivers = river_card.shape[1]
    owners = river_strength.shape[1]
    capacity = river_strength.shape[2]
    levels = lax.axis_size("depth")
    selector = (parent[0][:, None] == jnp.arange(node_count, dtype=jnp.int32)[None, :]).astype(
        jnp.float32
    )
    opp_rows = opp_strat[0, 0]
    own_rows = own_strat[0, 0]
    root_row = root_reach[0]
    every_select, every_opp = in_one_piece((selector[None], opp_rows[None]), "depth", 0, 2)
    current = every_opp[0] * root_row[None, :]
    stacked = [current]
    for level_index in range(1, levels):
        current = every_opp[level_index] * choose_parent(every_select[level_index], current)
        stacked.append(current)
    reach_rows = lax.dynamic_index_in_dim(
        jnp.stack(stacked), lax.axis_index("depth"), 0, keepdims=False
    )
    compatible = compatible_table(hand_cards)
    alive_mask = alive_rows(hand_cards, river_card[0])
    board_reach = (alive_mask[:, None, :] * reach_rows[None, :, :]).astype(jnp.bfloat16)
    target = board_owner[0] * capacity + board_slot[0]
    fetched = lax.all_to_all(river_strength[0], "board", split_axis=0, concat_axis=0, tiled=True)
    my_strength = jnp.take(fetched.reshape(owners * capacity, hand_count), target, axis=0)
    per_river = settle_boards(my_strength, board_reach, compatible)
    pot_scale = pot[0, 0] / (hand_count * rivers)
    showdown = pot_scale[:, None] * jnp.einsum(
        "rh,rkh->kh", alive_mask, per_river, precision=lax.Precision.HIGHEST
    )
    every_select, every_own, every_show = side_by_side(
        (selector[None], own_rows[None], showdown[None]), "depth", 0, 2
    )
    carried = jnp.zeros_like(showdown)
    collected = [None] * levels
    for level_index in reversed(range(levels)):
        collected[level_index] = carried
        carried = lift_to_parents(
            every_select[level_index], every_own[level_index] * (every_show[level_index] + carried)
        )
    incoming = lax.dynamic_index_in_dim(
        jnp.stack(collected), lax.axis_index("depth"), 0, keepdims=False
    )
    node_value = showdown + incoming
    return node_value[None, None]


def solution(mesh):
    placed = (
        P("board", None),
        P("board", "depth", None, None),
        P("board", "depth", None, None),
        P("depth", None),
        P("board", "depth", None),
        P(),
        P("board", None),
        P("board", None),
        P("board", None),
        P("board", None, None, None),
    )
    return jax.shard_map(
        body, mesh=mesh, in_specs=placed, out_specs=P("board", "depth", None, None), check_vma=False
    )
```

profile of v0, /device:TPU:2, one launch (start us, length us, event | category | flops | bytes accessed | tf_op | source)
XLA Modules:
  0.0 213.7 jit_solution(8258236134375970121)
XLA Ops:
  0.0 7.8 %all-to-all-start = ((f32[32,2,1326]{2,1,0:T(2,128)}), f32[32,2,1326]{2,1,0:T(2,128)S(1)}, u32[]{:S(2)}, u32[]{:S(2)}) async-start(f32[32,2,1326]{2,1,0:T(2,128)} %bitcast.251), calls=%async_computation | async-start | bytes 720896 | tf_op jit(solution)/shard_map/all_to_all | solution.py:124
  7.8 0.7 fusion.53
  8.5 0.7 compare_and_fusion.1
  9.1 0.7 fusion.52
  9.9 1.0 pad_maximum_fusion
  10.9 29.5 %all_gather.3 = f32[8,16,1342]{2,1,0:T(8,128)S(1)} all-gather(f32[1,16,1342]{2,1,0:T(8,128)S(1)} %pad_maximum_fusion), channel_id=1, replica_groups=mesh['depth'=8,'board'=32] {'depth'}, dimensions={0}, use_global_device_ids=true | all-gather | bytes 772992 | tf_op jit(solution)/shard_map/all_gather | solution.py:10
  40.4 0.7 reduce.4
  41.1 0.1 fusion.50
  41.2 0.3 bitcast_dynamic-update-slice_fusion.11
  41.5 0.2 bitcast_dynamic-update-slice_fusion.10
  41.8 0.2 bitcast_dynamic-update-slice_fusion.9
  42.0 0.2 bitcast_dynamic-update-slice_fusion.8
  42.2 0.2 bitcast_dynamic-update-slice_fusion.7
  42.5 0.2 bitcast_dynamic-update-slice_fusion.6
  42.7 0.2 fusion.14
  43.0 0.1 bitcast_convert_fusion
  43.1 1.2 multiply_convert_fusion
  44.2 3.3 %fusion.12 = bf16[1326,1326]{1,0:T(8,128)(2,1)} fusion(s32[1326]{0:T(1024)S(1)} %get-tuple-element.34, s32[1326]{0:T(1024)S(1)} %get-tuple-element.33), kind=kOutput, calls=%fused_computation.11 | convolution fusion | flops 186584096 | bytes 3527160 | tf_op jit(solution)/shard_map/dot_general | solution.py:43
  47.5 0.2 reshape.170
  47.8 0.6 gather_fusion
  48.4 0.1 broadcast_select_fusion
  48.5 125.9 %while.10 = (s32[]{:T(128)}, f32[26,16,1326]{2,1,0:T(8,128)S(1)}, bf16[26,16,1326]{2,1,0:T(8,128)(2,1)}, f32[26,1326]{1,0:T(8,128)S(1)}, bf16[1326,1326]{1,0:T(8,128)(2,1)}, /*index=5*/s32[]{:T(128)}) while((s32[]{:T(128)}, f32[26,16,1326]{2,1,0:T(8,128)S(1)}, bf16[26,16,1326]{2,1,0:T(8,128)(2,1)}, f32[26,1326]{1,0:T(8,128)S(1)}, ...), condition=%wide.region_1.2_spmd, body=%wide.region_0.1_spmd.sunk | while | flops 63297936 | bytes 3902905 | solution.py:68
  48.5 4.8 %fusion.65 = f32[26,16,1326]{2,1,0:T(8,128)S(1)} fusion(f32[26,16,1326]{2,1,0:T(8,128)S(1)} %get-tuple-element.97, s32[]{:T(128)} %get-tuple-element.96, bf16[1326,1326]{1,0:T(8,128)(2,1)} %get-tuple-element.106, f32[1326]{0:T(1024)S(1)} %dynamic-slice_reduce_fusion.2, bf16[26,16,1326]{2,1,0:T(8,128)(2,1)} %get-tuple-element.104), kind=kOutput, calls=%fused_computation.5.clone.1 | convolution fusion | flops 63297936 | bytes 3892224 | tf_op jit(solution)/shard_map/while/body/eval_jaxpr/dot_general | solution.py:58
  53.4 4.8 %fusion.65 = f32[26,16,1326]{2,1,0:T(8,128)S(1)} fusion(f32[26,16,1326]{2,1,0:T(8,128)S(1)} %get-tuple-element.97, s32[]{:T(128)} %get-tuple-element.96, bf16[1326,1326]{1,0:T(8,128)(2,1)} %get-tuple-element.106, f32[1326]{0:T(1024)S(1)} %dynamic-slice_reduce_fusion.2, bf16[26,16,1326]{2,1,0:T(8,128)(2,1)} %get-tuple-element.104), kind=kOutput, calls=%fused_computation.5.clone.1 | convolution fusion | flops 63297936 | bytes 3892224 | tf_op jit(solution)/shard_map/while/body/eval_jaxpr/dot_general | solution.py:58
  58.2 4.8 %fusion.65 = f32[26,16,1326]{2,1,0:T(8,128)S(1)} fusion(f32[26,16,1326]{2,1,0:T(8,128)S(1)} %get-tuple-element.97, s32[]{:T(128)} %get-tuple-element.96, bf16[1326,1326]{1,0:T(8,128)(2,1)} %get-tuple-element.106, f32[1326]{0:T(1024)S(1)} %dynamic-slice_reduce_fusion.2, bf16[26,16,1326]{2,1,0:T(8,128)(2,1)} %get-tuple-element.104), kind=kOutput, calls=%fused_computation.5.clone.1 | convolution fusion | flops 63297936 | bytes 3892224 | tf_op jit(solution)/shard_map/while/body/eval_jaxpr/dot_general | solution.py:58
  63.1 4.8 %fusion.65 = f32[26,16,1326]{2,1,0:T(8,128)S(1)} fusion(f32[26,16,1326]{2,1,0:T(8,128)S(1)} %get-tuple-element.97, s32[]{:T(128)} %get-tuple-element.96, bf16[1326,1326]{1,0:T(8,128)(2,1)} %get-tuple-element.106, f32[1326]{0:T(1024)S(1)} %dynamic-slice_reduce_fusion.2, bf16[26,16,1326]{2,1,0:T(8,128)(2,1)} %get-tuple-element.104), kind=kOutput, calls=%fused_computation.5.clone.1 | convolution fusion | flops 63297936 | bytes 3892224 | tf_op jit(solution)/shard_map/while/body/eval_jaxpr/dot_general | solution.py:58
  67.9 4.8 %fusion.65 = f32[26,16,1326]{2,1,0:T(8,128)S(1)} fusion(f32[26,16,1326]{2,1,0:T(8,128)S(1)} %get-tuple-element.97, s32[]{:T(128)} %get-tuple-element.96, bf16[1326,1326]{1,0:T(8,128)(2,1)} %get-tuple-element.106, f32[1326]{0:T(1024)S(1)} %dynamic-slice_reduce_fusion.2, bf16[26,16,1326]{2,1,0:T(8,128)(2,1)} %get-tuple-element.104), kind=kOutput, calls=%fused_computation.5.clone.1 | convolution fusion | flops 63297936 | bytes 3892224 | tf_op jit(solution)/shard_map/while/body/eval_jaxpr/dot_general | solution.py:58
  72.7 4.8 %fusion.65 = f32[26,16,1326]{2,1,0:T(8,128)S(1)} fusion(f32[26,16,1326]{2,1,0:T(8,128)S(1)} %get-tuple-element.97, s32[]{:T(128)} %get-tuple-element.96, bf16[1326,1326]{1,0:T(8,128)(2,1)} %get-tuple-element.106, f32[1326]{0:T(1024)S(1)} %dynamic-slice_reduce_fusion.2, bf16[26,16,1326]{2,1,0:T(8,128)(2,1)} %get-tuple-element.104), kind=kOutput, calls=%fused_computation.5.clone.1 | convolution fusion | flops 63297936 | bytes 3892224 | tf_op jit(solution)/shard_map/while/body/eval_jaxpr/dot_general | solution.py:58
  77.6 4.8 %fusion.65 = f32[26,16,1326]{2,1,0:T(8,128)S(1)} fusion(f32[26,16,1326]{2,1,0:T(8,128)S(1)} %get-tuple-element.97, s32[]{:T(128)} %get-tuple-element.96, bf16[1326,1326]{1,0:T(8,128)(2,1)} %get-tuple-element.106, f32[1326]{0:T(1024)S(1)} %dynamic-slice_reduce_fusion.2, bf16[26,16,1326]{2,1,0:T(8,128)(2,1)} %get-tuple-element.104), kind=kOutput, calls=%fused_computation.5.clone.1 | convolution fusion | flops 63297936 | bytes 3892224 | tf_op jit(solution)/shard_map/while/body/eval_jaxpr/dot_general | solution.py:58
  82.4 4.8 %fusion.65 = f32[26,16,1326]{2,1,0:T(8,128)S(1)} fusion(f32[26,16,1326]{2,1,0:T(8,128)S(1)} %get-tuple-element.97, s32[]{:T(128)} %get-tuple-element.96, bf16[1326,1326]{1,0:T(8,128)(2,1)} %get-tuple-element.106, f32[1326]{0:T(1024)S(1)} %dynamic-slice_reduce_fusion.2, bf16[26,16,1326]{2,1,0:T(8,128)(2,1)} %get-tuple-element.104), kind=kOutput, calls=%fused_computation.5.clone.1 | convolution fusion | flops 63297936 | bytes 3892224 | tf_op jit(solution)/shard_map/while/body/eval_jaxpr/dot_general | solution.py:58
  87.3 4.8 %fusion.65 = f32[26,16,1326]{2,1,0:T(8,128)S(1)} fusion(f32[26,16,1326]{2,1,0:T(8,128)S(1)} %get-tuple-element.97, s32[]{:T(128)} %get-tuple-element.96, bf16[1326,1326]{1,0:T(8,128)(2,1)} %get-tuple-element.106, f32[1326]{0:T(1024)S(1)} %dynamic-slice_reduce_fusion.2, bf16[26,16,1326]{2,1,0:T(8,128)(2,1)} %get-tuple-element.104), kind=kOutput, calls=%fused_computation.5.clone.1 | convolution fusion | flops 63297936 | bytes 3892224 | tf_op jit(solution)/shard_map/while/body/eval_jaxpr/dot_general | solution.py:58
  92.1 4.8 %fusion.65 = f32[26,16,1326]{2,1,0:T(8,128)S(1)} fusion(f32[26,16,1326]{2,1,0:T(8,128)S(1)} %get-tuple-element.97, s32[]{:T(128)} %get-tuple-element.96, bf16[1326,1326]{1,0:T(8,128)(2,1)} %get-tuple-element.106, f32[1326]{0:T(1024)S(1)} %dynamic-slice_reduce_fusion.2, bf16[26,16,1326]{2,1,0:T(8,128)(2,1)} %get-tuple-element.104), kind=kOutput, calls=%fused_computation.5.clone.1 | convolution fusion | flops 63297936 | bytes 3892224 | tf_op jit(solution)/shard_map/while/body/eval_jaxpr/dot_general | solution.py:58
  97.0 4.8 %fusion.65 = f32[26,16,1326]{2,1,0:T(8,128)S(1)} fusion(f32[26,16,1326]{2,1,0:T(8,128)S(1)} %get-tuple-element.97, s32[]{:T(128)} %get-tuple-element.96, bf16[1326,1326]{1,0:T(8,128)(2,1)} %get-tuple-element.106, f32[1326]{0:T(1024)S(1)} %dynamic-slice_reduce_fusion.2, bf16[26,16,1326]{2,1,0:T(8,128)(2,1)} %get-tuple-element.104), kind=kOutput, calls=%fused_computation.5.clone.1 | convolution fusion | flops 63297936 | bytes 3892224 | tf_op jit(solution)/shard_map/while/body/eval_jaxpr/dot_general | solution.py:58
  101.8 4.8 %fusion.65 = f32[26,16,1326]{2,1,0:T(8,128)S(1)} fusion(f32[26,16,1326]{2,1,0:T(8,128)S(1)} %get-tuple-element.97, s32[]{:T(128)} %get-tuple-element.96, bf16[1326,1326]{1,0:T(8,128)(2,1)} %get-tuple-element.106, f32[1326]{0:T(1024)S(1)} %dynamic-slice_reduce_fusion.2, bf16[26,16,1326]{2,1,0:T(8,128)(2,1)} %get-tuple-element.104), kind=kOutput, calls=%fused_computation.5.clone.1 | convolution fusion | flops 63297936 | bytes 3892224 | tf_op jit(solution)/shard_map/while/body/eval_jaxpr/dot_general | solution.py:58
  106.6 4.8 %fusion.65 = f32[26,16,1326]{2,1,0:T(8,128)S(1)} fusion(f32[26,16,1326]{2,1,0:T(8,128)S(1)} %get-tuple-element.97, s32[]{:T(128)} %get-tuple-element.96, bf16[1326,1326]{1,0:T(8,128)(2,1)} %get-tuple-element.106, f32[1326]{0:T(1024)S(1)} %dynamic-slice_reduce_fusion.2, bf16[26,16,1326]{2,1,0:T(8,128)(2,1)} %get-tuple-element.104), kind=kOutput, calls=%fused_computation.5.clone.1 | convolution fusion | flops 63297936 | bytes 3892224 | tf_op jit(solution)/shard_map/while/body/eval_jaxpr/dot_general | solution.py:58
  111.5 4.8 %fusion.65 = f32[26,16,1326]{2,1,0:T(8,128)S(1)} fusion(f32[26,16,1326]{2,1,0:T(8,128)S(1)} %get-tuple-element.97, s32[]{:T(128)} %get-tuple-element.96, bf16[1326,1326]{1,0:T(8,128)(2,1)} %get-tuple-element.106, f32[1326]{0:T(1024)S(1)} %dynamic-slice_reduce_fusion.2, bf16[26,16,1326]{2,1,0:T(8,128)(2,1)} %get-tuple-element.104), kind=kOutput, calls=%fused_computation.5.clone.1 | convolution fusion | flops 63297936 | bytes 3892224 | tf_op jit(solution)/shard_map/while/body/eval_jaxpr/dot_general | solution.py:58
  116.3 4.8 %fusion.65 = f32[26,16,1326]{2,1,0:T(8,128)S(1)} fusion(f32[26,16,1326]{2,1,0:T(8,128)S(1)} %get-tuple-element.97, s32[]{:T(128)} %get-tuple-element.96, bf16[1326,1326]{1,0:T(8,128)(2,1)} %get-tuple-element.106, f32[1326]{0:T(1024)S(1)} %dynamic-slice_reduce_fusion.2, bf16[26,16,1326]{2,1,0:T(8,128)(2,1)} %get-tuple-element.104), kind=kOutput, calls=%fused_computation.5.clone.1 | convolution fusion | flops 63297936 | bytes 3892224 | tf_op jit(solution)/shard_map/while/body/eval_jaxpr/dot_general | solution.py:58
  121.2 4.8 %fusion.65 = f32[26,16,1326]{2,1,0:T(8,128)S(1)} fusion(f32[26,16,1326]{2,1,0:T(8,128)S(1)} %get-tuple-element.97, s32[]{:T(128)} %get-tuple-element.96, bf16[1326,1326]{1,0:T(8,128)(2,1)} %get-tuple-element.106, f32[1326]{0:T(1024)S(1)} %dynamic-slice_reduce_fusion.2, bf16[26,16,1326]{2,1,0:T(8,128)(2,1)} %get-tuple-element.104), kind=kOutput, calls=%fused_computation.5.clone.1 | convolution fusion | flops 63297936 | bytes 3892224 | tf_op jit(solution)/shard_map/while/body/eval_jaxpr/dot_general | solution.py:58
  126.0 4.8 %fusion.65 = f32[26,16,1326]{2,1,0:T(8,128)S(1)} fusion(f32[26,16,1326]{2,1,0:T(8,128)S(1)} %get-tuple-element.97, s32[]{:T(128)} %get-tuple-element.96, bf16[1326,1326]{1,0:T(8,128)(2,1)} %get-tuple-element.106, f32[1326]{0:T(1024)S(1)} %dynamic-slice_reduce_fusion.2, bf16[26,16,1326]{2,1,0:T(8,128)(2,1)} %get-tuple-element.104), kind=kOutput, calls=%fused_computation.5.clone.1 | convolution fusion | flops 63297936 | bytes 3892224 | tf_op jit(solution)/shard_map/while/body/eval_jaxpr/dot_general | solution.py:58
  130.9 4.8 %fusion.65 = f32[26,16,1326]{2,1,0:T(8,128)S(1)} fusion(f32[26,16,1326]{2,1,0:T(8,128)S(1)} %get-tuple-element.97, s32[]{:T(128)} %get-tuple-element.96, bf16[1326,1326]{1,0:T(8,128)(2,1)} %get-tuple-element.106, f32[1326]{0:T(1024)S(1)} %dynamic-slice_reduce_fusion.2, bf16[26,16,1326]{2,1,0:T(8,128)(2,1)} %get-tuple-element.104), kind=kOutput, calls=%fused_computation.5.clone.1 | convolution fusion | flops 63297936 | bytes 3892224 | tf_op jit(solution)/shard_map/while/body/eval_jaxpr/dot_general | solution.py:58
  135.7 4.8 %fusion.65 = f32[26,16,1326]{2,1,0:T(8,128)S(1)} fusion(f32[26,16,1326]{2,1,0:T(8,128)S(1)} %get-tuple-element.97, s32[]{:T(128)} %get-tuple-element.96, bf16[1326,1326]{1,0:T(8,128)(2,1)} %get-tuple-element.106, f32[1326]{0:T(1024)S(1)} %dynamic-slice_reduce_fusion.2, bf16[26,16,1326]{2,1,0:T(8,128)(2,1)} %get-tuple-element.104), kind=kOutput, calls=%fused_computation.5.clone.1 | convolution fusion | flops 63297936 | bytes 3892224 | tf_op jit(solution)/shard_map/while/body/eval_jaxpr/dot_general | solution.py:58
  140.5 0.1 dynamic-slice_reduce_fusion.2
  140.6 4.8 %fusion.65 = f32[26,16,1326]{2,1,0:T(8,128)S(1)} fusion(f32[26,16,1326]{2,1,0:T(8,128)S(1)} %get-tuple-element.97, s32[]{:T(128)} %get-tuple-element.96, bf16[1326,1326]{1,0:T(8,128)(2,1)} %get-tuple-element.106, f32[1326]{0:T(1024)S(1)} %dynamic-slice_reduce_fusion.2, bf16[26,16,1326]{2,1,0:T(8,128)(2,1)} %get-tuple-element.104), kind=kOutput, calls=%fused_computation.5.clone.1 | convolution fusion | flops 63297936 | bytes 3892224 | tf_op jit(solution)/shard_map/while/body/eval_jaxpr/dot_general | solution.py:58
  145.4 4.8 %fusion.65 = f32[26,16,1326]{2,1,0:T(8,128)S(1)} fusion(f32[26,16,1326]{2,1,0:T(8,128)S(1)} %get-tuple-element.97, s32[]{:T(128)} %get-tuple-element.96, bf16[1326,1326]{1,0:T(8,128)(2,1)} %get-tuple-element.106, f32[1326]{0:T(1024)S(1)} %dynamic-slice_reduce_fusion.2, bf16[26,16,1326]{2,1,0:T(8,128)(2,1)} %get-tuple-element.104), kind=kOutput, calls=%fused_computation.5.clone.1 | convolution fusion | flops 63297936 | bytes 3892224 | tf_op jit(solution)/shard_map/while/body/eval_jaxpr/dot_general | solution.py:58
  150.2 0.1 dynamic-slice_reduce_fusion.2
  150.2 4.8 %fusion.65 = f32[26,16,1326]{2,1,0:T(8,128)S(1)} fusion(f32[26,16,1326]{2,1,0:T(8,128)S(1)} %get-tuple-element.97, s32[]{:T(128)} %get-tuple-element.96, bf16[1326,1326]{1,0:T(8,128)(2,1)} %get-tuple-element.106, f32[1326]{0:T(1024)S(1)} %dynamic-slice_reduce_fusion.2, bf16[26,16,1326]{2,1,0:T(8,128)(2,1)} %get-tuple-element.104), kind=kOutput, calls=%fused_computation.5.clone.1 | convolution fusion | flops 63297936 | bytes 3892224 | tf_op jit(solution)/shard_map/while/body/eval_jaxpr/dot_general | solution.py:58
  155.1 4.8 %fusion.65 = f32[26,16,1326]{2,1,0:T(8,128)S(1)} fusion(f32[26,16,1326]{2,1,0:T(8,128)S(1)} %get-tuple-element.97, s32[]{:T(128)} %get-tuple-element.96, bf16[1326,1326]{1,0:T(8,128)(2,1)} %get-tuple-element.106, f32[1326]{0:T(1024)S(1)} %dynamic-slice_reduce_fusion.2, bf16[26,16,1326]{2,1,0:T(8,128)(2,1)} %get-tuple-element.104), kind=kOutput, calls=%fused_computation.5.clone.1 | convolution fusion | flops 63297936 | bytes 3892224 | tf_op jit(solution)/shard_map/while/body/eval_jaxpr/dot_general | solution.py:58
  159.9 4.8 %fusion.65 = f32[26,16,1326]{2,1,0:T(8,128)S(1)} fusion(f32[26,16,1326]{2,1,0:T(8,128)S(1)} %get-tuple-element.97, s32[]{:T(128)} %get-tuple-element.96, bf16[1326,1326]{1,0:T(8,128)(2,1)} %get-tuple-element.106, f32[1326]{0:T(1024)S(1)} %dynamic-slice_reduce_fusion.2, bf16[26,16,1326]{2,1,0:T(8,128)(2,1)} %get-tuple-element.104), kind=kOutput, calls=%fused_computation.5.clone.1 | convolution fusion | flops 63297936 | bytes 3892224 | tf_op jit(solution)/shard_map/while/body/eval_jaxpr/dot_general | solution.py:58
  164.8 4.8 %fusion.65 = f32[26,16,1326]{2,1,0:T(8,128)S(1)} fusion(f32[26,16,1326]{2,1,0:T(8,128)S(1)} %get-tuple-element.97, s32[]{:T(128)} %get-tuple-element.96, bf16[1326,1326]{1,0:T(8,128)(2,1)} %get-tuple-element.106, f32[1326]{0:T(1024)S(1)} %dynamic-slice_reduce_fusion.2, bf16[26,16,1326]{2,1,0:T(8,128)(2,1)} %get-tuple-element.104), kind=kOutput, calls=%fused_computation.5.clone.1 | convolution fusion | flops 63297936 | bytes 3892224 | tf_op jit(solution)/shard_map/while/body/eval_jaxpr/dot_general | solution.py:58
  169.6 4.8 %fusion.65 = f32[26,16,1326]{2,1,0:T(8,128)S(1)} fusion(f32[26,16,1326]{2,1,0:T(8,128)S(1)} %get-tuple-element.97, s32[]{:T(128)} %get-tuple-element.96, bf16[1326,1326]{1,0:T(8,128)(2,1)} %get-tuple-element.106, f32[1326]{0:T(1024)S(1)} %dynamic-slice_reduce_fusion.2, bf16[26,16,1326]{2,1,0:T(8,128)(2,1)} %get-tuple-element.104), kind=kOutput, calls=%fused_computation.5.clone.1 | convolution fusion | flops 63297936 | bytes 3892224 | tf_op jit(solution)/shard_map/while/body/eval_jaxpr/dot_general | solution.py:58
  174.4 0.2 multiply_reduce_fusion
  174.6 0.1 multiply_bitcast_fusion
  174.7 0.6 copy-done
  175.3 0.1 concatenate.9
  175.5 0.1 broadcast_in_dim.40
  175.6 34.9 %all_to_all.10 = f32[8,1,16,2668]{3,2,1,0:T(8,128)S(1)} all-to-all(f32[8,1,16,2668]{3,2,1,0:T(8,128)S(1)} %broadcast_in_dim.40), channel_id=1, replica_groups=mesh['depth'=8,'board'=32] {'depth'}, dimensions={0} | all-to-all | bytes 2732032 | tf_op jit(solution)/shard_map/all_to_all | solution.py:22
  210.4 0.3 fusion.22
  210.8 0.3 fusion.27
  211.1 0.3 fusion.31
  211.5 0.3 fusion.35
  211.8 0.3 fusion.39
  212.1 0.3 fusion.43
  212.5 0.3 fusion.15
  212.9 0.7 fusion.48
  (44 shorter events, 1.4 us)
Async XLA Ops:
  0.0 41.5 %copy-start.1 = (s32[1326,2]{0,1:T(2,128)S(1)}, s32[1326,2]{0,1:T(2,128)}, u32[]{:S(2)}) copy-start(s32[1326,2]{0,1:T(2,128)} %param.17) | copy-start | bytes 31828
  0.0 41.5 %copy-start.3 = (f32[1,1,16]{2,1,0:T(1,128)S(1)}, f32[1,1,16]{2,1,0:T(1,128)}, u32[]{:S(2)}) copy-start(f32[1,1,16]{2,1,0:T(1,128)} %param.16) | copy-start | bytes 196
  0.0 42.9 %copy-start.2 = (s32[1,26]{1,0:T(1,128)S(1)}, s32[1,26]{1,0:T(1,128)}, u32[]{:S(2)}) copy-start(s32[1,26]{1,0:T(1,128)} %param.18) | copy-start | bytes 316
  0.0 47.5 %all-to-all-start = ((f32[32,2,1326]{2,1,0:T(2,128)}), f32[32,2,1326]{2,1,0:T(2,128)S(1)}, u32[]{:S(2)}, u32[]{:S(2)}) async-start(f32[32,2,1326]{2,1,0:T(2,128)} %bitcast.251), calls=%async_computation | async-start | bytes 720896 | tf_op jit(solution)/shard_map/all_to_all | solution.py:124
  174.4 0.9 copy-start
where the time goes:
time: 215 us; the launch traced here: 214 us
  matrix products  132 us (61%)
  blocking collectives  64.4 us (30%)
  starting transfers between devices  7.77 us (4%)
  other arithmetic  6.24 us (3%)
  local copies, waits for them, and re-layouts  3.14 us (1%)
    dot_general x26, matrix products, showdown_block(): lax.dot_general(reach_rows, sign_table, (((1,), (1,)), ((), ())), preferr...  124 us
    all_to_all x1, blocking collectives, sent_to_all(): return lax.all_to_all(copies, axis, split_axis=0, concat_axis=0, tiled=True)  34.9 us
    all_gather x1, blocking collectives, in_one_piece(): filled = lax.all_gather(both, axis, axis=dim, tiled=True)  29.5 us
    all_to_all x1, starting transfers between devices, body(): lax.all_to_all(river_strength[0], 'board', split_axis=0, concat_axis=0, t...  7.77 us
  transfers between devices with their start and end apart: 1, of which 0 were waited for; matrix products, arithmetic and copies ran while one was open for 5% of the time, Pallas kernels for 0%

commit v1 on v0

v1 whole, which is shorter than its diff:
```python
import jax
import jax.numpy as jnp
from jax import lax
from jax.experimental import pallas as pl
from jax.experimental.pallas import tpu as pltpu
from jax.sharding import PartitionSpec as P

LANES = 128
SCALE = 2.0**124
DEAD = 2.0**127
UNIT = 2.0**-25
LOW = 0.55
SPAN = 0.45
STEPS = 65535.0


def padded(n, to=LANES):
    return -(-n // to) * to


def pieces(x):
    first = x.astype(jnp.bfloat16)
    rest = x - first.astype(jnp.float32)
    second = rest.astype(jnp.bfloat16)
    third = (rest - second.astype(jnp.float32)).astype(jnp.bfloat16)
    return jnp.concatenate([first, second, third], axis=0)


def table_kernel(owner, slot, river, strengths, cards, compatible, table, rows, wide):
    rivers = owner.shape[1]
    hands = strengths.shape[2]
    width = rows.shape[1]
    blocks = width // LANES
    rows[...] = jnp.zeros(rows.shape, jnp.float32)
    first, second = cards[0:1, :], cards[1:2, :]
    dead_count = jnp.zeros((1, width), jnp.float32)
    for r in range(rivers):
        rows[r : r + 1, 0:hands] = strengths[owner[0, r], pl.ds(slot[0, r], 1), :] * SCALE
        card = river[0, r]
        dead = (first == card) | (second == card)
        rows[r : r + 1, :] = jnp.where(dead, DEAD, rows[r : r + 1, :])
        dead_count = dead_count + dead.astype(jnp.float32)
    rows[rivers : rivers + 1, :] = dead_count * UNIT

    def block(b, carry):
        at = pl.multiple_of(b * LANES, LANES)
        columns = rows[:, pl.ds(at, LANES)].T
        for r in range(rivers + 1):
            wide[r] = jnp.broadcast_to(columns[:, r : r + 1], (LANES, LANES))

        def tile(j, carry):
            to = pl.multiple_of(j * LANES, LANES)
            total = (rows[rivers : rivers + 1, pl.ds(to, LANES)] - wide[rivers]).astype(jnp.bfloat16)
            for r in range(rivers):
                apart = (wide[r] - rows[r : r + 1, pl.ds(to, LANES)]).astype(jnp.bfloat16)
                apart = jnp.maximum(apart, jnp.bfloat16(-UNIT))
                total = total + jnp.minimum(apart, jnp.bfloat16(UNIT))
            fits = compatible[pl.ds(at, LANES), pl.ds(to, LANES)]
            table[pl.ds(at, LANES), pl.ds(to, LANES)] = total * jnp.bfloat16(1.0 / UNIT) * fits
            return carry

        return lax.fori_loop(b, blocks, tile, carry)

    lax.fori_loop(0, blocks, block, 0)


def tree_kernel(level, table, shared, root, out, reach_rows, values, *, hands, scale):
    levels = shared.shape[0]
    nodes = shared.shape[1] // 2
    width = table.shape[0]
    blocks = width // LANES
    lane = lax.broadcasted_iota(jnp.int32, (nodes, 3 * nodes), 1)
    live = lax.broadcasted_iota(jnp.int32, (nodes, width), 1) < hands

    def decoded(coded):
        value = (coded.astype(jnp.float32) + 32768.0) * (SPAN / STEPS) + LOW
        return jnp.where(live, value, 0.0)

    def chosen(l):
        parent = shared[l, 0:nodes, hands : hands + 1].astype(jnp.int32)
        return (lane % nodes == parent).astype(jnp.bfloat16)

    current = decoded(shared[0, 0:nodes, :]) * root[...]
    reach_rows[0:nodes, :] = current.astype(jnp.bfloat16)
    for l in range(1, levels):
        above = jnp.dot(chosen(l), pieces(current), preferred_element_type=jnp.float32)
        current = decoded(shared[l, 0:nodes, :]) * above
        reach_rows[l * nodes : (l + 1) * nodes, :] = current.astype(jnp.bfloat16)

    values[...] = jnp.zeros(values.shape, jnp.float32)
    for b in range(blocks):
        at, end = b * LANES, (b + 1) * LANES
        values[:, at:end] += lax.dot_general(
            reach_rows[:, at:], table[at:end, at:], (((1,), (1,)), ((), ())),
            preferred_element_type=jnp.float32,
        )
        if end < width:
            values[:, end:] -= jnp.dot(
                reach_rows[:, at:end], table[at:end, end:], preferred_element_type=jnp.float32
            )

    carried = jnp.zeros((nodes, width), jnp.float32)
    for l in reversed(range(levels)):
        high = shared[l, 0:nodes, hands + 1 : hands + 2].astype(jnp.float32)
        low = shared[l, 0:nodes, hands + 2 : hands + 3].astype(jnp.float32)
        pot = (high + low * 2.0**-15) * 2.0**-12
        value = values[l * nodes : (l + 1) * nodes, :] * (pot * scale) + carried

        @pl.when(level[0] == l)
        def _():
            out[...] = value[:, 0:hands]

        if l > 0:
            weighted = decoded(shared[l, nodes : 2 * nodes, :]) * value
            carried = sum_to_parents(chosen(l), weighted, nodes)


def sum_to_parents(selector, weighted, nodes):
    picks = selector[:, 0:nodes].astype(jnp.float32).T.astype(jnp.bfloat16)
    picks = jnp.concatenate([picks, picks, picks], axis=1)
    return jnp.dot(picks, pieces(weighted), preferred_element_type=jnp.float32)


def coded(x, width):
    steps = jnp.round((x - LOW) * (STEPS / SPAN)) - 32768.0
    steps = jnp.clip(steps, -32768.0, 32767.0).astype(jnp.int16)
    return jnp.pad(steps, ((0, 0), (0, width - x.shape[1])))


def body(
    root_reach,
    opp_strat,
    own_strat,
    parent,
    pot,
    hand_cards,
    river_card,
    board_owner,
    board_slot,
    river_strength,
):
    hands = root_reach.shape[1]
    nodes = opp_strat.shape[2]
    rivers = river_card.shape[1]
    width = padded(hands + 3)
    levels = lax.axis_size("depth")

    fetched = lax.all_to_all(river_strength[0], "board", split_axis=0, concat_axis=0, tiled=True)

    scaled_pot = pot[0, 0] * 4096.0
    high = jnp.floor(scaled_pot)
    low = (scaled_pot - high) * 32768.0
    extra = jnp.stack([parent[0].astype(jnp.float32), high, low], axis=1).astype(jnp.int16)
    opp_coded = coded(opp_strat[0, 0], width)
    opp_coded = lax.dynamic_update_slice(opp_coded, extra, (0, hands))
    message = jnp.concatenate([opp_coded, coded(own_strat[0, 0], width)], axis=0)
    copies = jnp.broadcast_to(message, (levels, *message.shape))
    shared = lax.all_to_all(copies, "depth", split_axis=0, concat_axis=0, tiled=True)

    cards = jnp.pad(hand_cards.T, ((0, 0), (0, width - hands)), constant_values=-1)
    held = cards[None, :, :] == jnp.arange(64, dtype=jnp.int32)[:, None, None]
    onehot = (held[:, 0] | held[:, 1]).astype(jnp.bfloat16)
    together = lax.dot_general(
        onehot, onehot, (((0,), (0,)), ((), ())), preferred_element_type=jnp.float32
    )
    compatible = (together < 0.5).astype(jnp.bfloat16)

    smem = pl.BlockSpec(memory_space=pltpu.SMEM)
    vmem = pl.BlockSpec(memory_space=pltpu.VMEM)
    table = pl.pallas_call(
        table_kernel,
        out_shape=jax.ShapeDtypeStruct((width, width), jnp.bfloat16),
        in_specs=[smem, smem, smem, vmem, vmem, vmem],
        out_specs=vmem,
        scratch_shapes=[
            pltpu.VMEM((32, width), jnp.float32),
            pltpu.VMEM((rivers + 1, LANES, LANES), jnp.float32),
        ],
        name="sign_table",
    )(board_owner, board_slot, river_card, fetched, cards, compatible)

    root = jnp.pad(root_reach, ((0, 0), (0, width - hands)))
    level = lax.axis_index("depth").astype(jnp.int32).reshape(1)

    def tree(*refs):
        tree_kernel(*refs, hands=hands, scale=1.0 / (hands * rivers))

    node_value = pl.pallas_call(
        tree,
        out_shape=jax.ShapeDtypeStruct((nodes, hands), jnp.float32),
        in_specs=[smem, vmem, vmem, vmem],
        out_specs=vmem,
        scratch_shapes=[
            pltpu.VMEM((levels * nodes, width), jnp.bfloat16),
            pltpu.VMEM((levels * nodes, width), jnp.float32),
        ],
        name="tree_values",
    )(level, table, shared, root)
    return node_value[None, None]


def solution(mesh):
    placed = (
        P("board", None),
        P("board", "depth", None, None),
        P("board", "depth", None, None),
        P("depth", None),
        P("board", "depth", None),
        P(),
        P("board", None),
        P("board", None),
        P("board", None),
        P("board", None, None, None),
    )
    return jax.shard_map(
        body, mesh=mesh, in_specs=placed, out_specs=P("board", "depth", None, None), check_vma=False
    )
```

time: 215 us -> 65.1 us (0.30)
  the two profiles are of different devices: /device:TPU:2 before, /device:TPU:1 now
where the time goes in v1:
time: 65.1 us; the launch traced here: 64.7 us
  Pallas kernels  30.7 us (47%)
  starting transfers between devices  16.8 us (26%)
  waiting for transfers between devices  6.38 us (10%)
  local copies, waits for them, and re-layouts  4.31 us (7%)
  other arithmetic  3.3 us (5%)
  matrix products  3.18 us (5%)
    pallas_call x1, Pallas kernels, body(): pl.pallas_call(table_kernel, out_shape=jax.ShapeDtypeStruct((width, width...  23.2 us
    all_to_all x1, starting transfers between devices, body(): lax.all_to_all(river_strength[0], 'board', split_axis=0, concat_axis=0, t...  8.58 us
    all_to_all x1, starting transfers between devices, body(): lax.all_to_all(copies, 'depth', split_axis=0, concat_axis=0, tiled=True)  8.19 us
    pallas_call x1, Pallas kernels, body(): pl.pallas_call(tree, out_shape=jax.ShapeDtypeStruct((nodes, hands), jnp.f...  7.53 us
    all_to_all x1, waiting for transfers between devices, body(): lax.all_to_all(river_strength[0], 'board', split_axis=0, concat_axis=0, t...  6.38 us
    dot_general x1, matrix products, body(): lax.dot_general(onehot, onehot, (((0,), (0,)), ((), ())), preferred_eleme...  3.18 us
    convert_element_type x2, other arithmetic, coded(): steps = jnp.clip(steps, -32768.0, 32767.0).astype(jnp.int16)  1.84 us
  transfers between devices with their start and end apart: 2, of which 1 were waited for; matrix products, arithmetic and copies ran while one was open for 14% of the time, Pallas kernels for 36%

profile of v1, /device:TPU:1, one launch (start us, length us, event | category | flops | bytes accessed | tf_op | source)
XLA Modules:
  0.0 64.7 jit_solution(7168033569894806638)
XLA Ops:
  0.0 8.6 %all-to-all-start = ((f32[32,2,1326]{2,1,0:T(2,128)}), f32[32,2,1326]{2,1,0:T(2,128)S(1)}, u32[]{:S(2)}, u32[]{:S(2)}) async-start(f32[32,2,1326]{2,1,0:T(2,128)} %bitcast.16), calls=%async_computation | async-start | bytes 720896 | tf_op jit(solution)/shard_map/all_to_all | solution.py:148
  8.6 0.7 %floor_convert_fusion = (s16[16,1]{0,1:T(2,128)(2,1)S(1)}, s16[16,1]{0,1:T(2,128)(2,1)S(1)}) fusion(f32[1,1,16]{2,1,0:T(1,128)} %param.14), kind=kLoop, calls=%fused_computation.13 | loop fusion | flops 96 | bytes 128 | tf_op jit(solution)/shard_map/convert.1
  9.3 0.7 %convert_bitcast_fusion = s16[16,1]{0,1:T(2,128)(2,1)S(1)} fusion(s32[1,16]{1,0:T(1,128)} %param.13), kind=kLoop, calls=%fused_computation.16 | loop fusion | flops 32 | bytes 96 | tf_op jit(solution)/shard_map/convert_element_type | solution.py:153
  9.9 0.9 %fusion.4 = s16[16,1326]{1,0:T(8,128)(2,1)S(1)} fusion(f32[1,1,16,1326]{3,2,1,0:T(8,128)} %param.11), kind=kLoop, calls=%fused_computation.9 | loop fusion | flops 127296 | bytes 127296 | tf_op jit(solution)/shard_map/convert_element_type | solution.py:126
  10.8 0.9 %fusion.5 = s16[16,1326]{1,0:T(8,128)(2,1)S(1)} fusion(f32[1,1,16,1326]{3,2,1,0:T(8,128)} %param.12), kind=kLoop, calls=%fused_computation.10 | loop fusion | flops 127296 | bytes 127296 | tf_op jit(solution)/shard_map/convert_element_type | solution.py:126
  11.8 0.1 copy.12
  11.9 0.2 dynamic_update_slice.3
  12.2 6.4 %all-to-all-done.strengths = f32[32,2,1326]{2,1,0:T(2,128)S(1)} async-done(((f32[32,2,1326]{2,1,0:T(2,128)}), f32[32,2,1326]{2,1,0:T(2,128)S(1)}, u32[]{:S(2)}, u32[]{:S(2)}) %all-to-all-start) | async-done | bytes 339488 | tf_op jit(solution)/shard_map/all_to_all | solution.py:148
  18.5 0.0 copy-start.1
  18.5 1.1 %broadcast_in_dim.8 = s16[8,32,1408]{2,1,0:T(8,128)(2,1)} broadcast(s16[32,1408]{1,0:T(8,128)(2,1)S(1)} %pad_add_fusion), dimensions={1,2} | broadcast | bytes 811008 | tf_op jit(solution)/shard_map/broadcast_in_dim | solution.py:157
  19.6 8.2 %all-to-all-start.1 = ((s16[8,32,1408]{2,1,0:T(8,128)(2,1)}), s16[8,32,1408]{2,1,0:T(8,128)(2,1)S(1)}, u32[]{:S(2)}, u32[]{:S(2)}) async-start(s16[8,32,1408]{2,1,0:T(8,128)(2,1)} %broadcast_in_dim.8), calls=%async_computation.1 | async-start | bytes 1441792 | tf_op jit(solution)/shard_map/all_to_all | solution.py:158
  27.8 0.7 %pad.15.cards = s32[2,1408]{1,0:T(2,128)S(1)} pad(s32[2,1326]{1,0:T(2,128)} %bitcast.17, s32[]{:T(128)} %constant.10.clone.1), padding=0_0x0_82 | pad | bytes 21876 | tf_op jit(solution)/shard_map/jit(_pad)/pad | solution.py:160
  28.5 0.0 copy-start.2
  28.5 1.3 %pad.18.refs_3_ = f32[1,1408]{1,0:T(1,128)} pad(f32[1,1326]{1,0:T(1,128)} %param.10, f32[]{:T(128)} %constant.34.clone.1), padding=0_0x0_82 | pad | bytes 10940 | tf_op jit(solution)/shard_map/jit(_pad)/pad | solution.py:182
  29.8 0.1 iota_compare_fusion
  29.9 3.2 %fusion.compatible = bf16[1408,1408]{1,0:T(8,128)(2,1)} fusion(pred[64,2,1408]{2,0,1:T(32,128)(4,1)S(1)} %iota_compare_fusion), kind=kOutput, calls=%fused_computation.1 | convolution fusion | flops 257810432 | bytes 4145152 | tf_op jit(solution)/shard_map/dot_general | solution.py:163
  33.1 0.0 copy-done.1
  33.1 0.0 copy-done.2
  33.1 23.2 %sign_table.1.refs_1_ = bf16[1408,1408]{1,0:T(8,128)(2,1)} custom-call(s32[1,26]{1,0:T(1,128)} %owner.1, s32[1,26]{1,0:T(1,128)} %slot.1, s32[1,26]{1,0:T(1,128)} %river.1, f32[32,2,1326]{2,1,0:T(2,128)} %copy-done.1, s32[2,1408]{1,0:T(2,128)} %copy-done.2, bf16[1408,1408]{1,0:T(8,128)(2,1)} %fusion.compatible), custom_call_target="tpu_custom_call" | custom-call | tf_op jit(solution)/shard_map/sign_table/pallas_call | solution.py:170
  56.3 0.0 all-to-all-done.1.refs_2_
  56.3 0.0 copy-start
  56.3 0.9 %copy-done = s16[8,32,1408]{2,1,0:T(8,128)(2,1)} copy-done((s16[8,32,1408]{2,1,0:T(8,128)(2,1)}, s16[8,32,1408]{2,1,0:T(8,128)(2,1)S(1)}, u32[]{:S(2)}) %copy-start) | copy-done | bytes 720920
  57.2 7.5 %tree_values.1 = f32[16,1326]{1,0:T(8,128)} custom-call(s32[1]{0:T(128)} %bitcast.refs_0_, bf16[1408,1408]{1,0:T(8,128)(2,1)} %sign_table.1.refs_1_, s16[8,32,1408]{2,1,0:T(8,128)(2,1)} %copy-done, f32[1,1408]{1,0:T(1,128)} %pad.18.refs_3_), custom_call_target="tpu_custom_call" | custom-call | tf_op jit(solution)/shard_map/tree_values/pallas_call | solution.py:188
  (3 shorter events, 0.0 us)
Async XLA Ops:
  0.0 18.5 %all-to-all-start = ((f32[32,2,1326]{2,1,0:T(2,128)}), f32[32,2,1326]{2,1,0:T(2,128)S(1)}, u32[]{:S(2)}, u32[]{:S(2)}) async-start(f32[32,2,1326]{2,1,0:T(2,128)} %bitcast.16), calls=%async_computation | async-start | bytes 720896 | tf_op jit(solution)/shard_map/all_to_all | solution.py:148
  18.5 14.5 %copy-start.1 = (f32[32,2,1326]{2,1,0:T(2,128)}, f32[32,2,1326]{2,1,0:T(2,128)S(1)}, u32[]{:S(2)}) copy-start(f32[32,2,1326]{2,1,0:T(2,128)S(1)} %all-to-all-done.strengths) | copy-start | bytes 1018372
  19.6 36.7 %all-to-all-start.1 = ((s16[8,32,1408]{2,1,0:T(8,128)(2,1)}), s16[8,32,1408]{2,1,0:T(8,128)(2,1)S(1)}, u32[]{:S(2)}, u32[]{:S(2)}) async-start(s16[8,32,1408]{2,1,0:T(8,128)(2,1)} %broadcast_in_dim.8), calls=%async_computation.1 | async-start | bytes 1441792 | tf_op jit(solution)/shard_map/all_to_all | solution.py:158
  28.5 4.6 %copy-start.2 = (s32[2,1408]{1,0:T(2,128)}, s32[2,1408]{1,0:T(2,128)S(1)}, u32[]{:S(2)}) copy-start(s32[2,1408]{1,0:T(2,128)S(1)} %pad.15.cards) | copy-start | bytes 33796
  56.3 0.9 %copy-start = (s16[8,32,1408]{2,1,0:T(8,128)(2,1)}, s16[8,32,1408]{2,1,0:T(8,128)(2,1)S(1)}, u32[]{:S(2)}) copy-start(s16[8,32,1408]{2,1,0:T(8,128)(2,1)S(1)} %all-to-all-done.1.refs_2_) | copy-start | bytes 2162692
